TPU v7x, 256 devices: a whole 4x4x8 slice. The times are simulated.
256 devices in a mesh: row: 16 (over z, y_hi), col: 16 (over y_lo, x, core).
Axes of the slice: x: 4, y: 4 (y_hi: 2, y_lo: 2; y = y_hi * 2 + y_lo), z: 8, core: 2. Of those that a mesh axis runs over, the one named last changes fastest.
Arguments:
- amplitudes: bfloat16 [2048, 32768], P('row', 'col'), may hold values from -6 to 6
- amp_mask: int32 [64, 128], P('row', 'col'), may hold values from 0 to 1, as said below
- integrals: bfloat16 [16384, 32768], P('row', 'col'), may hold values from -0.0625 to 0.0625
- int_mask: int32 [64, 128], P('row', 'col'), may hold values 0 or 1
- occ_energy: float32 [2048], P('col'), may hold values from -1.5 to -0.5
- vir_energy: float32 [16384], P('row'), may hold values from 0.5 to 1.5
Outputs:
- residual: bfloat16 [2048, 16384], P('col', 'row')
Inputs may be any that keep to these rules, and one draw needn't show every extreme that they name: In every row of amp_mask, each aligned group of 8 consecutive entries holds exactly 4 ones.
All inputs are finite; a program needn't handle non-finite values. No bound on the sum of `int_mask` on one device may be relied on, other than what follows from the above.
Results may differ from a plain program's by a relative error of at most 0.001.
Values may be sent and summed in bfloat16 or wider, within the bound.
A program may use at most 64 MiB of HBM per device.

v0:
```python
import jax
import jax.numpy as jnp
from jax import lax
from jax.sharding import PartitionSpec as P

TILE = 256
IJ_BLK = 32


def expand_tiles(values, keep, rows_tile, cols_tile):
    nrow, ncol = keep.shape
    shaped = values.reshape(nrow, rows_tile, ncol, cols_tile)
    return (shaped * keep.astype(values.dtype)[:, None, :, None]).reshape(values.shape)


def contract(left, right):
    return lax.dot_general(
        left, right, (((1,), (1,)), ((), ())), preferred_element_type=jnp.float32
    )


def whole_sum(partial_value):
    return lax.psum_scatter(partial_value, "col", scatter_dimension=0, tiled=True)


def body(amplitudes, amp_mask, integrals, int_mask, occ_energy, vir_energy):
    int_used = expand_tiles(integrals, int_mask, TILE, TILE)
    amp_used = expand_tiles(amplitudes, amp_mask, IJ_BLK, TILE)
    partial_value = contract(lax.all_gather(amp_used, "row", axis=0, tiled=True), int_used)
    ladder = whole_sum(partial_value)
    denom = vir_energy[None, :] - occ_energy[:, None]
    return (ladder / denom).astype(jnp.bfloat16)


def solution(mesh):
    return jax.shard_map(
        body,
        mesh=mesh,
        in_specs=(
            P("row", "col"),
            P("row", "col"),
            P("row", "col"),
            P("row", "col"),
            P("col"),
            P("row"),
        ),
        out_specs=P("col", "row"),
        check_vma=False,
    )
```

profile of v0, /device:TPU:48, one launch (start us, length us, event | category | flops | bytes accessed | tf_op | source)
XLA Modules:
  0.0 246.2 jit_solution(13339371365637120035)
XLA Ops:
  6.5 0.0 all-gather.2.cloned.1.call-start
  6.5 0.7 convert_element_type.9
  7.2 0.1 mul.22
  7.3 0.1 copy.7
  7.5 2.0 mul.24
  9.5 0.0 all-gather.2.cloned.1.call-update
  9.5 0.0 reduce-scatter.2.cloned.1.call-start
  9.5 0.7 convert_element_type.10
  10.2 0.3 mul.25
  10.6 3.4 %copy.8 = bf16[128,8,8,256]{3,1,2,0:T(8,128)(2,1)} copy(bf16[128,8,8,256]{3,2,1,0:T(8,128)(2,1)S(1)} %bitcast.7) | data formatting | bytes 8388608
  14.0 129.4 %all-gather.2.cloned.1.call-done = bf16[2048,2048]{1,0:T(8,128)(2,1)} async-done(((bf16[128,2048]{1,0:T(8,128)(2,1)}), bf16[2048,2048]{1,0:T(8,128)(2,1)}) %all-gather.2.cloned.1.call-update) | async-done | bytes 8388624 | tf_op jit(solution)/shard_map/all_gather | solution.py:29
  143.3 15.8 %fusion = f32[2048,1024]{1,0:T(8,128)} fusion(bf16[2048,2048]{1,0:T(8,128)(2,1)} %all-gather.2.cloned.1.call-done, bf16[1024,2048]{1,0:T(8,128)(2,1)} %param.8, bf16[1024,2048]{1,0:T(8,128)(2,1)} %bitcast.8), kind=kOutput, calls=%fused_computation | convolution fusion | flops 8592031744 | bytes 25165824 | tf_op jit(solution)/shard_map/dot_general | solution.py:17
  159.1 0.0 copy-start
  159.1 0.0 copy-start.1
  159.1 0.0 reduce-scatter.2.cloned.1.call-update
  159.2 78.3 %reduce-scatter.2.cloned.1.call-done = f32[128,1024]{1,0:T(8,128)} async-done(((f32[2048,1024]{1,0:T(8,128)}), f32[128,1024]{1,0:T(8,128)}) %reduce-scatter.2.cloned.1.call-update) | async-done | bytes 524304 | tf_op jit(solution)/shard_map/reduce_scatter | solution.py:23
  237.4 0.0 copy-done
  237.5 0.0 copy-done.1
  237.5 1.9 divide_convert_fusion
Async XLA Ops:
  6.5 136.8 %all-gather.2.cloned.1.call-start = ((), (), s32[]{:S(2)}) async-start(), calls=%async_computation.1 | async-start | bytes 8912896 | tf_op jit(solution)/shard_map/all_gather | solution.py:29
  9.5 228.0 %reduce-scatter.2.cloned.1.call-start = ((), (), s32[]{:S(2)}) async-start(), calls=%async_computation.2 | async-start | bytes 8912896 | tf_op jit(solution)/shard_map/reduce_scatter | solution.py:23
  159.1 78.3 %copy-start = (f32[1024]{0:T(1024)S(1)}, f32[1024]{0:T(1024)}, u32[]{:S(2)}) copy-start(f32[1024]{0:T(1024)} %param.11) | copy-start | bytes 12292
  159.1 78.3 %copy-start.1 = (f32[128]{0:T(128)S(1)}, f32[128]{0:T(128)}, u32[]{:S(2)}) copy-start(f32[128]{0:T(128)} %param.10) | copy-start | bytes 1540
Sparse Core Ops, SparseCore 0:
  9.9 133.3 all-gather.1
  159.3 78.1 reduce-scatter.1
where the time goes:
time: 247 us; the launch traced here: 246 us
  waiting for transfers between devices  208 us (84%)
  matrix products  15.8 us (6%)
  between operations  13.4 us (5%)
  other arithmetic  5.27 us (2%)
  local copies, waits for them, and re-layouts  3.96 us (2%)
    all_gather x1, waiting for transfers between devices, body(): lax.all_gather(amp_used, 'row', axis=0, tiled=True)  129 us
    reduce_scatter x1, waiting for transfers between devices, whole_sum(): lax.psum_scatter(partial_value, 'col', scatter_dimension=0, tiled=True)  78.3 us
    dot_general x1, matrix products, contract(): lax.dot_general(left, right, (((1,), (1,)), ((), ())), preferred_element_...  15.8 us
  transfers between devices with their start and end apart: 2, of which 2 were waited for; matrix products, arithmetic and copies ran while one was open for 2% of the time, Pallas kernels for 0%

commit v1 on v0

v1 whole, which is shorter than its diff:
```python
import jax
import jax.numpy as jnp
from jax import lax
from jax.experimental import pallas as pl
from jax.experimental.pallas import tpu as pltpu
from jax.sharding import PartitionSpec as P

MESH = pl.DeviceIdType.MESH
TILE = 256
BLK = 32
KEPT = 4
NT = 8
NZ, NX = 8, 4
HALF = 64
CODE = 8 * HALF
PIECE = CODE + 16
ICH = 4


def kernel(amp_hbm, am, int_hbm, im, occ, vir, out,
           amp_v, int_v, own, pieces, dec, int_t, part, relay, roots, rows_in,
           amp_sem, int_sem, own_send, copy_sem, a_send, a_recv,
           t_send, t_recv, p_send, y_send, r1_recv, r2_recv, r3_recv):
    row, col = lax.axis_index("row"), lax.axis_index("col")
    z, yh = row // 2, lax.rem(row, 2)
    k, x, yl = lax.rem(col, 2), lax.rem(col // 2, NX), col // (2 * NX)
    z_up, z_dn = lax.rem(z + 1, NZ) * 2 + yh, lax.rem(z + NZ - 1, NZ) * 2 + yh
    x_up = (yl * NX + lax.rem(x + 1, NX)) * 2 + k
    x_dn = (yl * NX + lax.rem(x + NX - 1, NX)) * 2 + k
    core_other = (row, (yl * NX + x) * 2 + 1 - k)
    y_other = (row, ((1 - yl) * NX + x) * 2 + k)
    far_row = z * 2 + 1 - yh
    chip_col = (yl * NX + x) * 2

    def remote(src, dst, send, recv, device):
        return pltpu.make_async_remote_copy(
            src_ref=src, dst_ref=dst, send_sem=send, recv_sem=recv,
            device_id=device, device_id_type=MESH)

    amp_in = pltpu.make_async_copy(amp_hbm, amp_v, amp_sem)
    amp_in.start()
    width = NT * TILE // ICH
    int_in = [pltpu.make_async_copy(int_hbm.at[:, pl.ds(i * width, width)],
                                    int_v.at[:, pl.ds(i * width, width)], int_sem.at[i])
              for i in range(ICH)]
    for c in int_in:
        c.start()

    barrier = pltpu.get_barrier_semaphore()
    for device in ((z_up, col), (z_dn, col), (row, x_up), (row, x_dn), y_other, core_other,
                   (far_row, chip_col), (far_row, chip_col + 1)):
        pl.semaphore_signal(barrier, inc=1, device_id=device, device_id_type=MESH)

    amp_in.wait()
    row_id = lax.broadcasted_iota(jnp.int32, (16, 128), 0)
    for g in range(2):
        codes = jnp.zeros((16, 128), jnp.int32)
        for q in range(2):
            b = g * 2 + q
            count, code = jnp.int32(0), []
            for j in range(NT):
                m = am[b, j]
                count = count + m
                code.append(m * count)
                codes = jnp.where(row_id == q * NT + j, code[j], codes)
            for s in range(KEPT):
                for l in range(2):
                    acc = jnp.zeros((BLK, 128), jnp.bfloat16)
                    for j in range(s, s + KEPT + 1):
                        tile = amp_v[b * BLK:(b + 1) * BLK, j * TILE + l * 128:j * TILE + l * 128 + 128]
                        acc = jnp.where(code[j] == s + 1, tile, acc)
                    at = (s * 2 + l) * HALF + q * BLK
                    own[g, at:at + BLK, :] = acc
        own[g, CODE:CODE + 16, :] = codes.astype(jnp.float32).astype(jnp.bfloat16)

    pl.semaphore_wait(barrier, 8)

    far = [remote(own.at[g], pieces.at[0, g, k], own_send.at[0, g], a_recv.at[0, g, k],
                  (far_row, chip_col + yh)) for g in range(2)]
    near = [remote(own.at[g], pieces.at[0, g, k], own_send.at[1, g], a_recv.at[0, g, k],
                   core_other) for g in range(2)]
    keep = [pltpu.make_async_copy(own.at[g], pieces.at[0, g, k], a_recv.at[0, g, k])
            for g in range(2)]
    for g in range(2):
        far[g].start()

    @pl.when(k != yh)
    def _():
        for g in range(2):
            near[g].start()

    @pl.when(k == yh)
    def _():
        for g in range(2):
            keep[g].start()

    def turned(i, device):
        part_rows = pl.ds(pl.multiple_of(k * (NT * TILE) + i * width, width), width)
        return remote(int_t.at[part_rows], int_t.at[part_rows], t_send.at[i], t_recv.at[i], device)

    for i in range(ICH):
        int_in[i].wait()
        for jj in range(width // TILE):
            j = i * (width // TILE) + jj
            for a in range(4):
                tile = int_v[a * TILE:(a + 1) * TILE, j * TILE:(j + 1) * TILE]
                tile = jnp.where(im[a, j] != 0, tile, jnp.zeros_like(tile))
                at = pl.multiple_of(k * (NT * TILE) + j * TILE, TILE)
                int_t[pl.ds(at, TILE), a * TILE:(a + 1) * TILE] = tile.T
        turned(i, core_other).start()

    def forward(s, h):
        for g in range(2):
            to = (z_up, col) if g == 0 else (z_dn, col)
            remote(pieces.at[s, g, h], pieces.at[s, g, h], a_send.at[s, g, h],
                   a_recv.at[s, g, h], to).wait_recv()

            @pl.when(s + 1 < NZ)
            def _():
                after = lax.rem(s + 1, NZ)
                remote(pieces.at[s, g, h], pieces.at[after, g, h], a_send.at[s, g, h],
                       a_recv.at[after, g, h], to).start()

    forward(0, 0)
    for i in range(ICH):
        turned(i, core_other).wait_recv()

    def root_of(s, g):
        zs = lax.rem(z + NZ - s, NZ) if g == 0 else lax.rem(z + s, NZ)
        xr, yr = lax.rem(zs, NX), zs // NX
        return lax.rem(x + NX - xr, NX), yr

    def halves(s, g, w):
        return part.at[s, pl.ds(g * HALF + w * BLK, BLK), :]

    def compute(s):
        def spread(gh, _):
            g, h = gh // 2, lax.rem(gh, 2)
            for q in range(2):
                for j in range(NT):
                    code = jnp.broadcast_to(
                        pieces[s, g, h, CODE + q * NT + j:CODE + q * NT + j + 1, :], (BLK, 128))
                    for l in range(2):
                        acc = jnp.zeros((BLK, 128), jnp.bfloat16)
                        for t in range(max(0, j - KEPT), min(j, KEPT - 1) + 1):
                            at = (t * 2 + l) * HALF + q * BLK
                            acc = jnp.where(code == jnp.bfloat16(t + 1),
                                            pieces[s, g, h, at:at + BLK, :], acc)
                        to_row = pl.multiple_of(g * HALF + q * BLK, BLK)
                        to_col = pl.multiple_of(h * NT * TILE + j * TILE + l * 128, 128)
                        dec[pl.ds(to_row, BLK), pl.ds(to_col, 128)] = acc
            return 0

        lax.fori_loop(0, 4, spread, 0)
        for n in range(4):
            part[s, :, n * TILE:(n + 1) * TILE] = lax.dot_general(
                dec[...], int_t[:, n * TILE:(n + 1) * TILE], (((1,), (0,)), ((), ())),
                preferred_element_type=jnp.float32)

    def send_half(s, g, w, dst, recv, device):
        return remote(halves(s, g, w), dst, p_send.at[s, g, w], recv, device)

    def first(s):
        for g in range(2):
            d, yr = root_of(s, g)
            u, v = s * 2 + g, g * 2 + yr

            @pl.when(d == 2)
            def _():
                send_half(s, g, 0, relay.at[u], r1_recv.at[u], (row, x_dn)).start()
                send_half(s, g, 1, relay.at[u], r1_recv.at[u], (row, x_up)).start()

            @pl.when(d == 1)
            def _():
                send_half(s, g, 1, roots.at[v, 0, 1], r2_recv.at[v, 0, 1], (row, x_dn)).start()

            @pl.when(d == 3)
            def _():
                send_half(s, g, 0, roots.at[v, 1, 0], r2_recv.at[v, 1, 0], (row, x_up)).start()

    def second(s):
        for g in range(2):
            d, yr = root_of(s, g)
            u, v = s * 2 + g, g * 2 + yr

            @pl.when(d == 1)
            def _():
                send_half(s, g, 0, relay.at[u], r1_recv.at[u], (row, x_dn)).wait_recv()
                halves(s, g, 0)[...] += relay[u]
                send_half(s, g, 0, roots.at[v, 0, 0], r2_recv.at[v, 0, 0], (row, x_dn)).start()

            @pl.when(d == 3)
            def _():
                send_half(s, g, 1, relay.at[u], r1_recv.at[u], (row, x_up)).wait_recv()
                halves(s, g, 1)[...] += relay[u]
                send_half(s, g, 1, roots.at[v, 1, 1], r2_recv.at[v, 1, 1], (row, x_up)).start()

    def cross(s, g):
        whole = part.at[s, pl.ds(g * HALF, HALF), :]
        return remote(whole, rows_in.at[g], y_send.at[s, g], r3_recv.at[g], y_other)

    def third(s):
        for g in range(2):
            d, yr = root_of(s, g)
            v = g * 2 + yr

            @pl.when(d == 0)
            def _():
                for w in range(2):
                    for side in range(2):
                        send_half(s, g, w, roots.at[v, side, w], r2_recv.at[v, side, w],
                                  (row, x_dn)).wait_recv()
                    halves(s, g, w)[...] += roots[v, 0, w] + roots[v, 1, w]

                @pl.when(yr != yl)
                def _():
                    cross(s, g).start()

    def fourth(s):
        for g in range(2):
            d, yr = root_of(s, g)

            @pl.when(jnp.logical_and(d == 0, yr == yl))
            def _():
                cross(s, g).wait_recv()
                occ_col = jnp.broadcast_to(occ[...], (128, 128)).T
                for n in range(8):
                    cols = slice(n * 128, (n + 1) * 128)
                    total = part[s, g * HALF:(g + 1) * HALF, cols] + rows_in[g, :, cols]
                    denom = vir[:, cols] - occ_col[g * HALF:(g + 1) * HALF, :]
                    out[g * HALF:(g + 1) * HALF, cols] = (total / denom).astype(jnp.bfloat16)

    def step(t, _):
        @pl.when(t < NZ)
        def _():
            forward(t, 1)
            compute(t)
            first(t)

        @pl.when(t + 1 < NZ)
        def _():
            forward(t + 1, 0)

        @pl.when(jnp.logical_and(t >= 1, t - 1 < NZ))
        def _():
            second(t - 1)

        @pl.when(jnp.logical_and(t >= 2, t - 2 < NZ))
        def _():
            third(t - 2)

        @pl.when(t >= 3)
        def _():
            fourth(t - 3)

        return 0

    lax.fori_loop(0, NZ + 3, step, 0)

    for g in range(2):
        far[g].wait_send()

    @pl.when(k != yh)
    def _():
        for g in range(2):
            near[g].wait_send()

    for i in range(ICH):
        turned(i, core_other).wait_send()

    def drain(s, _):
        for g in range(2):
            @pl.when(s + 1 < NZ)
            def _():
                for h in range(2):
                    remote(pieces.at[s, g, h], pieces.at[s, g, h], a_send.at[s, g, h],
                           a_recv.at[s, g, h], (z_up, col)).wait_send()

            d, yr = root_of(s, g)

            @pl.when(d != 0)
            def _():
                for w in range(2):
                    send_half(s, g, w, relay.at[0], r1_recv.at[0], (row, x_dn)).wait_send()

            @pl.when(jnp.logical_and(d == 0, yr != yl))
            def _():
                cross(s, g).wait_send()
        return 0

    lax.fori_loop(0, NZ, drain, 0)


def body(amplitudes, amp_mask, integrals, int_mask, occ_energy, vir_energy):
    nij, ncd = amplitudes.shape
    nab = integrals.shape[0]
    dma = pltpu.SemaphoreType.DMA
    vmem = pl.BlockSpec(memory_space=pltpu.VMEM)
    smem = pl.BlockSpec(memory_space=pltpu.SMEM)
    hbm = pl.BlockSpec(memory_space=pl.ANY)
    return pl.pallas_call(
        kernel,
        out_shape=jax.ShapeDtypeStruct((nij, nab), jnp.bfloat16),
        in_specs=[hbm, smem, hbm, smem, vmem, vmem],
        out_specs=vmem,
        scratch_shapes=[
            pltpu.VMEM((nij, ncd), jnp.bfloat16),
            pltpu.VMEM((nab, ncd), jnp.bfloat16),
            pltpu.VMEM((2, PIECE, 128), jnp.bfloat16),
            pltpu.VMEM((NZ, 2, 2, PIECE, 128), jnp.bfloat16),
            pltpu.VMEM((nij, 2 * ncd), jnp.bfloat16),
            pltpu.VMEM((2 * ncd, nab), jnp.bfloat16),
            pltpu.VMEM((NZ, nij, nab), jnp.float32),
            pltpu.VMEM((2 * NZ, BLK, nab), jnp.float32),
            pltpu.VMEM((4, 2, 2, BLK, nab), jnp.float32),
            pltpu.VMEM((2, HALF, nab), jnp.float32),
            dma, dma((ICH,)), dma((2, 2)), dma, dma((NZ, 2, 2)), dma((NZ, 2, 2)),
            dma((ICH,)), dma((ICH,)), dma((NZ, 2, 2)), dma((NZ, 2)),
            dma((2 * NZ,)), dma((4, 2, 2)), dma((2,)),
        ],
        compiler_params=pltpu.CompilerParams(
            collective_id=0, has_side_effects=True, vmem_limit_bytes=60 * 1024 * 1024),
    )(amplitudes, amp_mask, integrals, int_mask, occ_energy[None, :], vir_energy[None, :])


def solution(mesh):
    return jax.shard_map(
        body,
        mesh=mesh,
        in_specs=(
            P("row", "col"),
            P("row", "col"),
            P("row", "col"),
            P("row", "col"),
            P("col"),
            P("row"),
        ),
        out_specs=P("col", "row"),
        check_vma=False,
    )
```

time: 247 us -> 84.8 us (0.34)
  the two profiles are of different devices: /device:TPU:48 before, /device:TPU:32 now
where the time goes in v1:
time: 84.8 us; the launch traced here: 84.6 us
  Pallas kernels  83 us (98%)
  local copies, waits for them, and re-layouts  1.67 us (2%)
    pallas_call x1, Pallas kernels, body(): pl.pallas_call(kernel, out_shape=jax.ShapeDtypeStruct((nij, nab), jnp.bfl...  83 us

profile of v1, /device:TPU:32, one launch (start us, length us, event | category | flops | bytes accessed | tf_op | source)
XLA Modules:
  0.0 84.6 jit_solution(7952935211135446029)
XLA Ops:
  0.0 83.0 %shard_map.64 = bf16[128,1024]{1,0:T(8,128)(2,1)} custom-call(bf16[128,2048]{1,0:T(8,128)(2,1)} %amp_hbm.1, s32[4,8]{1,0:T(4,128)} %am.1, bf16[1024,2048]{1,0:T(8,128)(2,1)} %int_hbm.1, s32[4,8]{1,0:T(4,128)} %im.1, f32[1,128]{1,0:T(1,128)} %bitcast.3, f32[1,1024]{1,0:T(1,128)} %bitcast.2), custom_call_target="tpu_custom_call" | custom-call | tf_op jit(solution)/shard_map/pallas_call | solution.py:301
  83.0 1.7 %copy.8 = bf16[128,1024]{1,0:T(8,128)(2,1)} copy(bf16[128,1024]{1,0:T(8,128)(2,1)} %shard_map.64) | data formatting | bytes 524288

commit v2 on v1

--- a/solution.py
+++ b/solution.py
@@ -14,12 +14,14 @@
 HALF = 64
 CODE = 8 * HALF
 PIECE = CODE + 16
+NEAR = 3
+LAG = (2, 4, 6)
 ICH = 4
 
 
 def kernel(amp_hbm, am, int_hbm, im, occ, vir, out,
            amp_v, int_v, own, pieces, dec, int_t, part, relay, roots, rows_in,
-           amp_sem, int_sem, own_send, copy_sem, a_send, a_recv,
+           amp_sem, int_sem, own_send, a_send, a_recv, far_send,
            t_send, t_recv, p_send, y_send, r1_recv, r2_recv, r3_recv):
     row, col = lax.axis_index("row"), lax.axis_index("col")
     z, yh = row // 2, lax.rem(row, 2)
@@ -94,6 +96,44 @@
         for g in range(2):
             keep[g].start()
 
+    def onward(src, s, g, h):
+        to = (z_up, col) if g == 0 else (z_dn, col)
+        after = lax.rem(s + 1, NZ)
+        return remote(src, pieces.at[after, g, h], a_send.at[s, g, h], a_recv.at[after, g, h], to)
+
+    def over(s, g, h):
+        return remote(pieces.at[s, g, h], pieces.at[s, g, h], far_send.at[s, g, h],
+                      a_recv.at[s, g, h], (far_row, col))
+
+    def arrived(s, g, h):
+        remote(pieces.at[s, g, h], pieces.at[s, g, h], a_send.at[s, g, h], a_recv.at[s, g, h],
+               (z_up, col)).wait_recv()
+
+    home = k == yh
+
+    def goes_on(s):
+        return jnp.logical_and(s + 1 < NZ, jnp.logical_or(home, s >= NEAR))
+
+    def goes_over(s):
+        return jnp.logical_and(home, jnp.logical_and(s >= 1, s <= NEAR))
+
+    def forward(s, h):
+        for g in range(2):
+            arrived(s, g, h)
+
+            @pl.when(goes_on(s))
+            def _():
+                onward(pieces.at[s, g, h], s, g, h).start()
+
+            @pl.when(goes_over(s))
+            def _():
+                over(s, g, h).start()
+
+    @pl.when(home)
+    def _():
+        for g in range(2):
+            onward(own.at[g], 0, g, k).start()
+
     def turned(i, device):
         part_rows = pl.ds(pl.multiple_of(k * (NT * TILE) + i * width, width), width)
         return remote(int_t.at[part_rows], int_t.at[part_rows], t_send.at[i], t_recv.at[i], device)
@@ -108,20 +148,23 @@
                 at = pl.multiple_of(k * (NT * TILE) + j * TILE, TILE)
                 int_t[pl.ds(at, TILE), a * TILE:(a + 1) * TILE] = tile.T
         turned(i, core_other).start()
-
-    def forward(s, h):
-        for g in range(2):
-            to = (z_up, col) if g == 0 else (z_dn, col)
-            remote(pieces.at[s, g, h], pieces.at[s, g, h], a_send.at[s, g, h],
-                   a_recv.at[s, g, h], to).wait_recv()
-
-            @pl.when(s + 1 < NZ)
-            def _():
-                after = lax.rem(s + 1, NZ)
-                remote(pieces.at[s, g, h], pieces.at[after, g, h], a_send.at[s, g, h],
-                       a_recv.at[after, g, h], to).start()
-
-    forward(0, 0)
+        if i == 0:
+            @pl.when(home)
+            def _():
+                for g in range(2):
+                    arrived(0, g, 1 - k)
+                    onward(pieces.at[0, g, 1 - k], 0, g, 1 - k).start()
+
+    @pl.when(home)
+    def _():
+        for g in range(2):
+            arrived(0, g, k)
+
+    @pl.when(jnp.logical_not(home))
+    def _():
+        forward(0, 0)
+        forward(0, 1)
+
     for i in range(ICH):
         turned(i, core_other).wait_recv()
 
@@ -233,7 +276,6 @@
     def step(t, _):
         @pl.when(t < NZ)
         def _():
-            forward(t, 1)
             compute(t)
             first(t)
 
@@ -241,21 +283,18 @@
         def _():
             forward(t + 1, 0)
 
-        @pl.when(jnp.logical_and(t >= 1, t - 1 < NZ))
+        for lag, job in zip(LAG, (second, third, fourth)):
+            @pl.when(jnp.logical_and(t >= lag, t - lag < NZ))
+            def _():
+                job(t - lag)
+
+        @pl.when(t + 1 < NZ)
         def _():
-            second(t - 1)
-
-        @pl.when(jnp.logical_and(t >= 2, t - 2 < NZ))
-        def _():
-            third(t - 2)
-
-        @pl.when(t >= 3)
-        def _():
-            fourth(t - 3)
+            forward(t + 1, 1)
 
         return 0
 
-    lax.fori_loop(0, NZ + 3, step, 0)
+    lax.fori_loop(0, NZ + LAG[2], step, 0)
 
     for g in range(2):
         far[g].wait_send()
@@ -270,11 +309,15 @@
 
     def drain(s, _):
         for g in range(2):
-            @pl.when(s + 1 < NZ)
+            @pl.when(goes_on(s))
             def _():
                 for h in range(2):
-                    remote(pieces.at[s, g, h], pieces.at[s, g, h], a_send.at[s, g, h],
-                           a_recv.at[s, g, h], (z_up, col)).wait_send()
+                    onward(pieces.at[s, g, h], s, g, h).wait_send()
+
+            @pl.when(goes_over(s))
+            def _():
+                for h in range(2):
+                    over(s, g, h).wait_send()
 
             d, yr = root_of(s, g)
 
@@ -314,7 +357,7 @@
             pltpu.VMEM((2 * NZ, BLK, nab), jnp.float32),
             pltpu.VMEM((4, 2, 2, BLK, nab), jnp.float32),
             pltpu.VMEM((2, HALF, nab), jnp.float32),
-            dma, dma((ICH,)), dma((2, 2)), dma, dma((NZ, 2, 2)), dma((NZ, 2, 2)),
+            dma, dma((ICH,)), dma((2, 2)), dma((NZ, 2, 2)), dma((NZ, 2, 2)), dma((NZ, 2, 2)),
             dma((ICH,)), dma((ICH,)), dma((NZ, 2, 2)), dma((NZ, 2)),
             dma((2 * NZ,)), dma((4, 2, 2)), dma((2,)),
         ],

time: 84.8 us -> 74.8 us (0.88)
  the two profiles are of different devices: /device:TPU:32 before, /device:TPU:48 now
where the time goes in v2:
time: 74.8 us; the launch traced here: 74.6 us
  Pallas kernels  72.9 us (97%)
  local copies, waits for them, and re-layouts  1.67 us (2%)
    pallas_call x1, Pallas kernels, body(): pl.pallas_call(kernel, out_shape=jax.ShapeDtypeStruct((nij, nab), jnp.bfl...  72.9 us
    unnamed x1, local copies, waits for them, and re-layouts  1.67 us

profile of v2, /device:TPU:48, one launch (start us, length us, event | category | flops | bytes accessed | tf_op | source)
XLA Modules:
  0.0 74.6 jit_solution(11485083441557053513)
XLA Ops:
  0.0 72.9 %shard_map.64 = bf16[128,1024]{1,0:T(8,128)(2,1)} custom-call(bf16[128,2048]{1,0:T(8,128)(2,1)} %amp_hbm.1, s32[4,8]{1,0:T(4,128)} %am.1, bf16[1024,2048]{1,0:T(8,128)(2,1)} %int_hbm.1, s32[4,8]{1,0:T(4,128)} %im.1, f32[1,128]{1,0:T(1,128)} %bitcast.3, f32[1,1024]{1,0:T(1,128)} %bitcast.2), custom_call_target="tpu_custom_call" | custom-call | tf_op jit(solution)/shard_map/pallas_call | solution.py:344
  73.0 1.7 %copy.8 = bf16[128,1024]{1,0:T(8,128)(2,1)} copy(bf16[128,1024]{1,0:T(8,128)(2,1)} %shard_map.64) | data formatting | bytes 524288

commit v3 on v2

--- a/solution.py
+++ b/solution.py
@@ -16,6 +16,7 @@
 PIECE = CODE + 16
 NEAR = 3
 LAG = (2, 4, 6)
+CUTS = ((0, 272), (272, 256))
 ICH = 4
 
 
@@ -77,39 +78,57 @@
 
     pl.semaphore_wait(barrier, 8)
 
-    far = [remote(own.at[g], pieces.at[0, g, k], own_send.at[0, g], a_recv.at[0, g, k],
-                  (far_row, chip_col + yh)) for g in range(2)]
-    near = [remote(own.at[g], pieces.at[0, g, k], own_send.at[1, g], a_recv.at[0, g, k],
-                   core_other) for g in range(2)]
-    keep = [pltpu.make_async_copy(own.at[g], pieces.at[0, g, k], a_recv.at[0, g, k])
-            for g in range(2)]
-    for g in range(2):
-        far[g].start()
-
-    @pl.when(k != yh)
-    def _():
-        for g in range(2):
-            near[g].start()
-
-    @pl.when(k == yh)
-    def _():
-        for g in range(2):
-            keep[g].start()
-
-    def onward(src, s, g, h):
+    def own_cut(g, u):
+        return own.at[g, pl.ds(*CUTS[u]), :]
+
+    def cut(s, g, h, u):
+        return pieces.at[s, g, h, pl.ds(*CUTS[u]), :]
+
+    def far(g, u):
+        return remote(own_cut(g, u), cut(0, g, k, u), own_send.at[0, g, u],
+                      a_recv.at[0, g, k, u], (far_row, chip_col + yh))
+
+    def near(g, u):
+        return remote(own_cut(g, u), cut(0, g, k, u), own_send.at[1, g, u],
+                      a_recv.at[0, g, k, u], core_other)
+
+    def keep(g, u):
+        return pltpu.make_async_copy(own_cut(g, u), cut(0, g, k, u), a_recv.at[0, g, k, u])
+
+    def onward(src, s, g, h, u):
         to = (z_up, col) if g == 0 else (z_dn, col)
         after = lax.rem(s + 1, NZ)
-        return remote(src, pieces.at[after, g, h], a_send.at[s, g, h], a_recv.at[after, g, h], to)
-
-    def over(s, g, h):
-        return remote(pieces.at[s, g, h], pieces.at[s, g, h], far_send.at[s, g, h],
-                      a_recv.at[s, g, h], (far_row, col))
-
-    def arrived(s, g, h):
-        remote(pieces.at[s, g, h], pieces.at[s, g, h], a_send.at[s, g, h], a_recv.at[s, g, h],
+        return remote(src, cut(after, g, h, u), a_send.at[s, g, h, u], a_recv.at[after, g, h, u],
+                      to)
+
+    def over(s, g, h, u):
+        return remote(cut(s, g, h, u), cut(s, g, h, u), far_send.at[s, g, h, u],
+                      a_recv.at[s, g, h, u], (far_row, col))
+
+    def arrived(s, g, h, u):
+        remote(cut(s, g, h, u), cut(s, g, h, u), a_send.at[s, g, h, u], a_recv.at[s, g, h, u],
                (z_up, col)).wait_recv()
 
     home = k == yh
+    each = [(u, g) for u in range(2) for g in range(2)]
+
+    @pl.when(home)
+    def _():
+        for u, g in each:
+            onward(own_cut(g, u), 0, g, k, u).start()
+
+    @pl.when(k != yh)
+    def _():
+        for u, g in each:
+            near(g, u).start()
+
+    for u, g in each:
+        far(g, u).start()
+
+    @pl.when(home)
+    def _():
+        for u, g in each:
+            keep(g, u).start()
 
     def goes_on(s):
         return jnp.logical_and(s + 1 < NZ, jnp.logical_or(home, s >= NEAR))
@@ -118,21 +137,16 @@
         return jnp.logical_and(home, jnp.logical_and(s >= 1, s <= NEAR))
 
     def forward(s, h):
-        for g in range(2):
-            arrived(s, g, h)
+        for u, g in each:
+            arrived(s, g, h, u)
 
             @pl.when(goes_on(s))
             def _():
-                onward(pieces.at[s, g, h], s, g, h).start()
+                onward(cut(s, g, h, u), s, g, h, u).start()
 
             @pl.when(goes_over(s))
             def _():
-                over(s, g, h).start()
-
-    @pl.when(home)
-    def _():
-        for g in range(2):
-            onward(own.at[g], 0, g, k).start()
+                over(s, g, h, u).start()
 
     def turned(i, device):
         part_rows = pl.ds(pl.multiple_of(k * (NT * TILE) + i * width, width), width)
@@ -151,14 +165,14 @@
         if i == 0:
             @pl.when(home)
             def _():
-                for g in range(2):
-                    arrived(0, g, 1 - k)
-                    onward(pieces.at[0, g, 1 - k], 0, g, 1 - k).start()
+                for u, g in each:
+                    arrived(0, g, 1 - k, u)
+                    onward(cut(0, g, 1 - k, u), 0, g, 1 - k, u).start()
 
     @pl.when(home)
     def _():
-        for g in range(2):
-            arrived(0, g, k)
+        for u, g in each:
+            arrived(0, g, k, u)
 
     @pl.when(jnp.logical_not(home))
     def _():
@@ -296,13 +310,13 @@
 
     lax.fori_loop(0, NZ + LAG[2], step, 0)
 
-    for g in range(2):
-        far[g].wait_send()
+    for u, g in each:
+        far(g, u).wait_send()
 
     @pl.when(k != yh)
     def _():
-        for g in range(2):
-            near[g].wait_send()
+        for u, g in each:
+            near(g, u).wait_send()
 
     for i in range(ICH):
         turned(i, core_other).wait_send()
@@ -312,12 +326,14 @@
             @pl.when(goes_on(s))
             def _():
                 for h in range(2):
-                    onward(pieces.at[s, g, h], s, g, h).wait_send()
+                    for u in range(2):
+                        onward(cut(s, g, h, u), s, g, h, u).wait_send()
 
             @pl.when(goes_over(s))
             def _():
                 for h in range(2):
-                    over(s, g, h).wait_send()
+                    for u in range(2):
+                        over(s, g, h, u).wait_send()
 
             d, yr = root_of(s, g)
 
@@ -357,7 +373,8 @@
             pltpu.VMEM((2 * NZ, BLK, nab), jnp.float32),
             pltpu.VMEM((4, 2, 2, BLK, nab), jnp.float32),
             pltpu.VMEM((2, HALF, nab), jnp.float32),
-            dma, dma((ICH,)), dma((2, 2)), dma((NZ, 2, 2)), dma((NZ, 2, 2)), dma((NZ, 2, 2)),
+            dma, dma((ICH,)), dma((2, 2, 2)), dma((NZ, 2, 2, 2)), dma((NZ, 2, 2, 2)),
+            dma((NZ, 2, 2, 2)),
             dma((ICH,)), dma((ICH,)), dma((NZ, 2, 2)), dma((NZ, 2)),
             dma((2 * NZ,)), dma((4, 2, 2)), dma((2,)),
         ],

time: 74.8 us -> 74.4 us (level); the launches traced: 74.6 us -> 73 us
  Pallas kernels: 72.9 us -> 71.3 us
    pallas_call x1, Pallas kernels: 72.9 us -> 71.3 us  [body(): pl.pallas_call(kernel, out_shape=jax.ShapeDtypeStruct((nij, nab), jnp.bfl...]
where the time goes in v3:
time: 74.4 us; the launch traced here: 73 us
  Pallas kernels  71.3 us (96%)
  local copies, waits for them, and re-layouts  1.67 us (2%)
    pallas_call x1, Pallas kernels, body(): pl.pallas_call(kernel, out_shape=jax.ShapeDtypeStruct((nij, nab), jnp.bfl...  71.3 us
    unnamed x1, local copies, waits for them, and re-layouts  1.67 us

profile of v3, /device:TPU:48, one launch (start us, length us, event | category | flops | bytes accessed | tf_op | source)
XLA Modules:
  0.0 73.0 jit_solution(15433398792372294663)
XLA Ops:
  0.0 71.3 %shard_map.64 = bf16[128,1024]{1,0:T(8,128)(2,1)} custom-call(bf16[128,2048]{1,0:T(8,128)(2,1)} %amp_hbm.1, s32[4,8]{1,0:T(4,128)} %am.1, bf16[1024,2048]{1,0:T(8,128)(2,1)} %int_hbm.1, s32[4,8]{1,0:T(4,128)} %im.1, f32[1,128]{1,0:T(1,128)} %bitcast.3, f32[1,1024]{1,0:T(1,128)} %bitcast.2), custom_call_target="tpu_custom_call" | custom-call | tf_op jit(solution)/shard_map/pallas_call | solution.py:360
  71.3 1.7 %copy.8 = bf16[128,1024]{1,0:T(8,128)(2,1)} copy(bf16[128,1024]{1,0:T(8,128)(2,1)} %shard_map.64) | data formatting | bytes 524288

commit v4 on v3

--- a/solution.py
+++ b/solution.py
@@ -17,6 +17,7 @@
 NEAR = 3
 LAG = (2, 4, 6)
 CUTS = ((0, 272), (272, 256))
+COLS = 2
 ICH = 4
 
 
@@ -187,8 +188,13 @@
         xr, yr = lax.rem(zs, NX), zs // NX
         return lax.rem(x + NX - xr, NX), yr
 
-    def halves(s, g, w):
-        return part.at[s, pl.ds(g * HALF + w * BLK, BLK), :]
+    span = part.shape[2] // COLS
+
+    def side(c):
+        return pl.ds(c * span, span)
+
+    def halves(s, g, w, c):
+        return part.at[s, pl.ds(g * HALF + w * BLK, BLK), side(c)]
 
     def compute(s):
         def spread(gh, _):
@@ -214,64 +220,77 @@
                 dec[...], int_t[:, n * TILE:(n + 1) * TILE], (((1,), (0,)), ((), ())),
                 preferred_element_type=jnp.float32)
 
-    def send_half(s, g, w, dst, recv, device):
-        return remote(halves(s, g, w), dst, p_send.at[s, g, w], recv, device)
+    def send_half(s, g, w, c, dst, recv, device):
+        return remote(halves(s, g, w, c), dst, p_send.at[s, g, w, c], recv, device)
+
+    def to_relay(s, g, w, c, device):
+        return send_half(s, g, w, c, relay.at[s * 2 + g, :, side(c)], r1_recv.at[s * 2 + g, c],
+                         (row, device))
+
+    def to_root(s, g, w, c, yr, come, device):
+        i = g * 2 + yr
+        return send_half(s, g, w, c, roots.at[i, come, w, :, side(c)],
+                         r2_recv.at[i, come, w, c], (row, device))
 
     def first(s):
         for g in range(2):
             d, yr = root_of(s, g)
-            u, v = s * 2 + g, g * 2 + yr
 
             @pl.when(d == 2)
             def _():
-                send_half(s, g, 0, relay.at[u], r1_recv.at[u], (row, x_dn)).start()
-                send_half(s, g, 1, relay.at[u], r1_recv.at[u], (row, x_up)).start()
+                for c in range(COLS):
+                    to_relay(s, g, 0, c, x_dn).start()
+                    to_relay(s, g, 1, c, x_up).start()
 
             @pl.when(d == 1)
             def _():
-                send_half(s, g, 1, roots.at[v, 0, 1], r2_recv.at[v, 0, 1], (row, x_dn)).start()
+                for c in range(COLS):
+                    to_root(s, g, 1, c, yr, 0, x_dn).start()
 
             @pl.when(d == 3)
             def _():
-                send_half(s, g, 0, roots.at[v, 1, 0], r2_recv.at[v, 1, 0], (row, x_up)).start()
+                for c in range(COLS):
+                    to_root(s, g, 0, c, yr, 1, x_up).start()
 
     def second(s):
         for g in range(2):
             d, yr = root_of(s, g)
-            u, v = s * 2 + g, g * 2 + yr
 
             @pl.when(d == 1)
             def _():
-                send_half(s, g, 0, relay.at[u], r1_recv.at[u], (row, x_dn)).wait_recv()
-                halves(s, g, 0)[...] += relay[u]
-                send_half(s, g, 0, roots.at[v, 0, 0], r2_recv.at[v, 0, 0], (row, x_dn)).start()
+                for c in range(COLS):
+                    to_relay(s, g, 0, c, x_dn).wait_recv()
+                    halves(s, g, 0, c)[...] += relay[s * 2 + g, :, side(c)]
+                    to_root(s, g, 0, c, yr, 0, x_dn).start()
 
             @pl.when(d == 3)
             def _():
-                send_half(s, g, 1, relay.at[u], r1_recv.at[u], (row, x_up)).wait_recv()
-                halves(s, g, 1)[...] += relay[u]
-                send_half(s, g, 1, roots.at[v, 1, 1], r2_recv.at[v, 1, 1], (row, x_up)).start()
-
-    def cross(s, g):
-        whole = part.at[s, pl.ds(g * HALF, HALF), :]
-        return remote(whole, rows_in.at[g], y_send.at[s, g], r3_recv.at[g], y_other)
+                for c in range(COLS):
+                    to_relay(s, g, 1, c, x_up).wait_recv()
+                    halves(s, g, 1, c)[...] += relay[s * 2 + g, :, side(c)]
+                    to_root(s, g, 1, c, yr, 1, x_up).start()
+
+    def cross(s, g, c):
+        whole = part.at[s, pl.ds(g * HALF, HALF), side(c)]
+        return remote(whole, rows_in.at[g, :, side(c)], y_send.at[s, g, c], r3_recv.at[g, c],
+                      y_other)
 
     def third(s):
         for g in range(2):
             d, yr = root_of(s, g)
-            v = g * 2 + yr
 
             @pl.when(d == 0)
             def _():
-                for w in range(2):
-                    for side in range(2):
-                        send_half(s, g, w, roots.at[v, side, w], r2_recv.at[v, side, w],
-                                  (row, x_dn)).wait_recv()
-                    halves(s, g, w)[...] += roots[v, 0, w] + roots[v, 1, w]
-
-                @pl.when(yr != yl)
-                def _():
-                    cross(s, g).start()
+                for c in range(COLS):
+                    for w in range(2):
+                        for come in range(2):
+                            to_root(s, g, w, c, yr, come, x_dn).wait_recv()
+                        halves(s, g, w, c)[...] += (roots[g * 2 + yr, 0, w, :, side(c)]
+                                                    + roots[g * 2 + yr, 1, w, :, side(c)])
+
+                    @pl.when(yr != yl)
+                    def _():
+                        cross(s, g, c).start()
 
     def fourth(s):
         for g in range(2):
@@ -279,13 +298,14 @@
 
             @pl.when(jnp.logical_and(d == 0, yr == yl))
             def _():
-                cross(s, g).wait_recv()
                 occ_col = jnp.broadcast_to(occ[...], (128, 128)).T
-                for n in range(8):
-                    cols = slice(n * 128, (n + 1) * 128)
-                    total = part[s, g * HALF:(g + 1) * HALF, cols] + rows_in[g, :, cols]
-                    denom = vir[:, cols] - occ_col[g * HALF:(g + 1) * HALF, :]
-                    out[g * HALF:(g + 1) * HALF, cols] = (total / denom).astype(jnp.bfloat16)
+                for c in range(COLS):
+                    cross(s, g, c).wait_recv()
+                    for n in range(8 // COLS):
+                        cols = slice(c * span + n * 128, c * span + (n + 1) * 128)
+                        total = part[s, g * HALF:(g + 1) * HALF, cols] + rows_in[g, :, cols]
+                        denom = vir[:, cols] - occ_col[g * HALF:(g + 1) * HALF, :]
+                        out[g * HALF:(g + 1) * HALF, cols] = (total / denom).astype(jnp.bfloat16)
 
     def step(t, _):
         @pl.when(t < NZ)
@@ -340,11 +360,13 @@
             @pl.when(d != 0)
             def _():
                 for w in range(2):
-                    send_half(s, g, w, relay.at[0], r1_recv.at[0], (row, x_dn)).wait_send()
+                    for c in range(COLS):
+                        to_relay(s, g, w, c, x_dn).wait_send()
 
             @pl.when(jnp.logical_and(d == 0, yr != yl))
             def _():
-                cross(s, g).wait_send()
+                for c in range(COLS):
+                    cross(s, g, c).wait_send()
         return 0
 
     lax.fori_loop(0, NZ, drain, 0)
@@ -375,8 +397,8 @@
             pltpu.VMEM((2, HALF, nab), jnp.float32),
             dma, dma((ICH,)), dma((2, 2, 2)), dma((NZ, 2, 2, 2)), dma((NZ, 2, 2, 2)),
             dma((NZ, 2, 2, 2)),
-            dma((ICH,)), dma((ICH,)), dma((NZ, 2, 2)), dma((NZ, 2)),
-            dma((2 * NZ,)), dma((4, 2, 2)), dma((2,)),
+            dma((ICH,)), dma((ICH,)), dma((NZ, 2, 2, COLS)), dma((NZ, 2, COLS)),
+            dma((2 * NZ, COLS)), dma((4, 2, 2, COLS)), dma((2, COLS)),
         ],
         compiler_params=pltpu.CompilerParams(
             collective_id=0, has_side_effects=True, vmem_limit_bytes=60 * 1024 * 1024),

time: 74.4 us -> 74 us (level)
  no operation moved by 1% of the time
where the time goes in v4:
time: 74 us; the launch traced here: 73.2 us
  Pallas kernels  71.5 us (97%)
  local copies, waits for them, and re-layouts  1.67 us (2%)
    pallas_call x1, Pallas kernels, body(): pl.pallas_call(kernel, out_shape=jax.ShapeDtypeStruct((nij, nab), jnp.bfl...  71.5 us
    unnamed x1, local copies, waits for them, and re-layouts  1.67 us

profile of v4, /device:TPU:48, one launch (start us, length us, event | category | flops | bytes accessed | tf_op | source)
XLA Modules:
  0.0 73.2 jit_solution(3289352153081642810)
XLA Ops:
  0.0 71.5 %shard_map.64 = bf16[128,1024]{1,0:T(8,128)(2,1)} custom-call(bf16[128,2048]{1,0:T(8,128)(2,1)} %amp_hbm.1, s32[4,8]{1,0:T(4,128)} %am.1, bf16[1024,2048]{1,0:T(8,128)(2,1)} %int_hbm.1, s32[4,8]{1,0:T(4,128)} %im.1, f32[1,128]{1,0:T(1,128)} %bitcast.3, f32[1,1024]{1,0:T(1,128)} %bitcast.2), custom_call_target="tpu_custom_call" | custom-call | tf_op jit(solution)/shard_map/pallas_call | solution.py:382
  71.5 1.7 %copy.8 = bf16[128,1024]{1,0:T(8,128)(2,1)} copy(bf16[128,1024]{1,0:T(8,128)(2,1)} %shard_map.64) | data formatting | bytes 524288
